TPU v7x, 256 devices: a whole 4x4x8 slice. The times are simulated.
256 devices in a mesh: cfg: 2 (over x_lo), wide: 32 (over x_hi, z, core), narrow: 4 (over y).
Axes of the slice: x: 4 (x_hi: 2, x_lo: 2; x = x_hi * 2 + x_lo), y: 4, z: 8, core: 2. Of those that a mesh axis runs over, the one named last changes fastest.
Arguments:
- hidden: bfloat16 [2, 4096, 3072], P('cfg', 'wide', 'narrow'), may hold values from -120 to 120
- split_table: int32 [32], replicated, may hold values from 1 to 128, 2048 in all
- modulation: float32 [8, 3072], P(None, 'narrow'), may hold values from -4 to 4
- expand_weight: bfloat16 [3072, 12288], P('narrow', 'wide'), may hold values from -0.109375 to 0.109375
- contract_weight: bfloat16 [12288, 3072], P('wide', 'narrow'), may hold values from -0.0546875 to 0.0546875
- output_weight: bfloat16 [3072, 64], P('narrow'), may hold values from -0.109375 to 0.109375
- latent: float32 [4096, 64], P('wide'), may hold values from -6 to 6
- timestep: int32 [1], replicated, may hold values from 20 to 499
Outputs:
- layer_out: bfloat16 [2, 4096, 3072], P('cfg', 'wide', 'narrow')
- clean_latent: float32 [4096, 64], P('wide')
Inputs may be any that keep to these rules, and one draw needn't show every extreme that they name: `split_table`: the entries sum to 2048, and the largest is exactly 128.
All inputs are finite; a program needn't handle non-finite values.
Results may differ from a plain program's by a relative error of at most 0.0056.
Values may be sent and summed in bfloat16 or wider, within the bound.
A program may use at most 64 MiB of HBM per device.

v0:
```python
import jax
import jax.numpy as jnp
from jax import lax
from jax.sharding import PartitionSpec as P

D = 3072
TEXT = 226
norm_eps = 1e-05
guidance = 6.0


def alpha_table():
    steps_index = jnp.arange(1000, dtype=jnp.int32)
    start_root = 0.00085**0.5
    end_root = 0.012**0.5
    roots = start_root + (end_root - start_root) * steps_index.astype(jnp.float32) / 999.0
    return (steps_index, jnp.cumprod(1.0 - roots * roots))


def feature_norm(values, shifts, scaling):
    totals, squares = lax.psum(
        (jnp.sum(values, -1, keepdims=True), jnp.sum(values * values, -1, keepdims=True)), "narrow"
    )
    average = totals / D
    variance = squares / D - average * average
    return (values - average) * lax.rsqrt(variance + norm_eps) * (1.0 + scaling) + shifts


def on_device(
    hidden, split_table, modulation, expand_weight, contract_weight, output_weight, latent, timestep
):
    capacity = hidden.shape[1]
    wide_index = lax.axis_index("wide")
    table_index = jnp.arange(split_table.shape[0], dtype=jnp.int32)
    offset = jnp.sum(jnp.where(table_index < wide_index, split_table, 0))
    own_count = jnp.sum(jnp.where(table_index == wide_index, split_table, 0))
    slot_index = jnp.arange(capacity, dtype=jnp.int32)
    position = offset + slot_index
    slot_live = slot_index < own_count
    is_text = slot_live & (position < TEXT)
    is_video = slot_live & (position >= TEXT)
    text_column = is_text[:, None]
    shifts = jnp.where(text_column, modulation[3], modulation[0])
    scaling = jnp.where(text_column, modulation[4], modulation[1])
    gating = jnp.where(text_column, modulation[5], modulation[2])
    values = hidden[0].astype(jnp.float32)
    normed = feature_norm(values, shifts, scaling).astype(jnp.bfloat16)
    hidden_part = jnp.dot(
        lax.all_gather(normed, "wide", axis=0, tiled=True),
        expand_weight,
        preferred_element_type=jnp.float32,
    )
    hidden_pre = lax.psum(hidden_part, "narrow")
    activated = jax.nn.gelu(hidden_pre, approximate=True).astype(jnp.bfloat16)
    ff_result = lax.psum_scatter(
        jnp.dot(activated, contract_weight, preferred_element_type=jnp.float32),
        "wide",
        scatter_dimension=0,
        tiled=True,
    )
    layer_out = jnp.where(slot_live[:, None], values + gating * ff_result, 0.0).astype(jnp.bfloat16)
    final_in = layer_out.astype(jnp.float32)
    final_normed = feature_norm(final_in, modulation[6], modulation[7]).astype(jnp.bfloat16)
    velocity_part = jnp.dot(final_normed, output_weight, preferred_element_type=jnp.float32)
    copy_weight = jnp.where(lax.axis_index("cfg") == 0, guidance, 1.0 - guidance)
    guided = lax.psum(velocity_part * copy_weight, ("cfg", "narrow"))
    steps_index, alpha_bar = alpha_table()
    alpha_now = jnp.sum(jnp.where(steps_index == timestep[0], alpha_bar, 0.0))
    clean_latent = jnp.where(
        is_video[:, None], jnp.sqrt(alpha_now) * latent - jnp.sqrt(1.0 - alpha_now) * guided, 0.0
    )
    return (layer_out[None], clean_latent)


def solution(mesh):
    return jax.shard_map(
        on_device,
        mesh=mesh,
        in_specs=(
            P("cfg", "wide", "narrow"),
            P(),
            P(None, "narrow"),
            P("narrow", "wide"),
            P("wide", "narrow"),
            P("narrow", None),
            P("wide", None),
            P(),
        ),
        out_specs=(P("cfg", "wide", "narrow"), P("wide", None)),
        check_vma=False,
    )
```

profile of v0, /device:TPU:2, one launch (start us, length us, event | category | flops | bytes accessed | tf_op | source)
XLA Modules:
  0.0 493.6 jit_solution(13559903819700724804)
XLA Ops:
  7.2 0.0 copy-start
  7.2 0.0 all-gather.2.cloned.1.call-start
  7.2 1.1 convert_reduce_fusion.1
  8.3 1.1 fusion.21
  9.4 1.1 add_reduce_fusion
  10.5 1.3 fusion.34
  11.8 1.3 compare_and_fusion.1
  13.1 10.7 %all-reduce.2 = (f32[128,1]{0,1:T(1,128)S(1)}, f32[128,1]{0,1:T(1,128)S(1)}) all-reduce(f32[128,1]{0,1:T(1,128)S(1)} %bitcast.48, f32[128,1]{0,1:T(1,128)S(1)} %bitcast.47), channel_id=1, replica_groups=mesh['cfg'=2,'wide'=32,'narrow'=4] {'narrow'}, use_global_device_ids=true, to_apply=%region_5.6 | all-reduce | flops 256 | bytes 2048 | tf_op jit(solution)/shard_map/psum | solution.py:21
  23.8 1.8 fusion.20
  25.7 0.0 all-gather.2.cloned.1.call-update
  25.7 0.0 all-reduce.5.cloned.1.call-start
  25.7 94.3 %all-gather.2.cloned.1.call-done = bf16[4096,768]{1,0:T(8,128)(2,1)} async-done(((bf16[128,768]{1,0:T(8,128)(2,1)}), bf16[4096,768]{1,0:T(8,128)(2,1)}) %all-gather.2.cloned.1.call-update) | async-done | bytes 6291472 | tf_op jit(solution)/shard_map/all_gather | solution.py:49
  120.1 9.0 %fusion.41 = f32[4096,384]{1,0:T(8,128)} fusion(bf16[4096,768]{1,0:T(8,128)(2,1)} %all-gather.2.cloned.1.call-done, bf16[768,384]{1,0:T(8,128)(2,1)} %param.11), kind=kOutput, calls=%fused_computation.70 | convolution fusion | flops 2415919104 | bytes 13172736 | tf_op jit(solution)/shard_map/dot_general | solution.py:48
  129.0 0.0 all-reduce.5.cloned.1.call-update
  129.1 0.0 reduce-scatter.2.cloned.1.call-start
  129.1 129.7 %all-reduce.5.cloned.1.call-done = f32[4096,384]{1,0:T(8,128)} async-done(((f32[4096,384]{1,0:T(8,128)}), f32[4096,384]{1,0:T(8,128)}) %all-reduce.5.cloned.1.call-update) | async-done | bytes 6291472 | tf_op jit(solution)/shard_map/psum | solution.py:53
  258.8 0.0 copy-done
  258.8 11.8 %fusion.8 = f32[4096,768]{1,0:T(8,128)} fusion(bf16[384,768]{1,0:T(8,128)(2,1)S(1)} %copy-done, f32[4096,384]{1,0:T(8,128)} %all-reduce.5.cloned.1.call-done), kind=kOutput, calls=%fused_computation.9 | convolution fusion | flops 2430074880 | bytes 19464192 | tf_op jit(solution)/shard_map/dot_general | solution.py:56
  270.6 0.0 copy-start.1
  270.6 0.0 copy-start.4
  270.6 0.0 copy-start.3
  270.6 0.0 reduce-scatter.2.cloned.1.call-update
  270.7 0.3 reduce-window.9
  271.0 0.1 slice.40
  271.7 0.1 slice_reduce_fusion
  271.8 0.1 multiply_bitcast_fusion
  271.9 0.7 select_reduce_fusion
  274.0 0.7 iota_compare_fusion.1
  274.7 1.3 compare_and_fusion
  275.9 167.3 %reduce-scatter.2.cloned.1.call-done = f32[128,768]{1,0:T(8,128)} async-done(((f32[4096,768]{1,0:T(8,128)}), f32[128,768]{1,0:T(8,128)}) %reduce-scatter.2.cloned.1.call-update) | async-done | bytes 393232 | tf_op jit(solution)/shard_map/reduce_scatter | solution.py:55
  443.2 0.0 copy-done.1
  443.2 1.3 convert_reduce_fusion
  444.5 0.0 copy-start.2
  444.5 10.5 %all-reduce.1 = (f32[128,1]{0,1:T(1,128)S(1)}, f32[128,1]{0,1:T(1,128)S(1)}) all-reduce(f32[128,1]{0,1:T(1,128)S(1)} %bitcast.50, f32[128,1]{0,1:T(1,128)S(1)} %bitcast.49), channel_id=1, replica_groups=mesh['cfg'=2,'wide'=32,'narrow'=4] {'narrow'}, use_global_device_ids=true, to_apply=%region_14.15 | all-reduce | flops 256 | bytes 2048 | tf_op jit(solution)/shard_map/psum | solution.py:21
  455.0 0.0 copy-done.4
  455.0 0.3 convolution_multiply_fusion
  455.3 31.1 %psum.47 = f32[128,64]{0,1:T(8,128)S(1)} all-reduce(f32[128,64]{0,1:T(8,128)S(1)} %convolution_multiply_fusion), channel_id=1, replica_groups=mesh['cfg'=2,'wide'=32,'narrow'=4] {'cfg','narrow'}, use_global_device_ids=true, to_apply=%region_15.16 | all-reduce | flops 8192 | bytes 65536 | tf_op jit(solution)/shard_map/psum | solution.py:66
  486.4 0.0 copy-done.3
  486.4 0.6 subtract_select_fusion
  487.1 0.0 copy-done.2
  (5 shorter events, 0.1 us)
Async XLA Ops:
  7.2 251.7 %copy-start = (bf16[384,768]{1,0:T(8,128)(2,1)S(1)}, bf16[384,768]{1,0:T(8,128)(2,1)}, u32[]{:S(2)}) copy-start(bf16[384,768]{1,0:T(8,128)(2,1)} %param.12) | copy-start | bytes 1769476
  7.2 112.9 %all-gather.2.cloned.1.call-start = ((), (), s32[]{:S(2)}) async-start(), calls=%async_computation.1 | async-start | bytes 6488064 | tf_op jit(solution)/shard_map/all_gather | solution.py:49
  25.7 233.1 %all-reduce.5.cloned.1.call-start = ((), (), s32[]{:S(2)}) async-start(), calls=%async_computation.2 | async-start | bytes 12582912 | tf_op jit(solution)/shard_map/psum | solution.py:53
  129.1 314.2 %reduce-scatter.2.cloned.1.call-start = ((), (), s32[]{:S(2)}) async-start(), calls=%async_computation.3 | async-start | bytes 12976128 | tf_op jit(solution)/shard_map/reduce_scatter | solution.py:55
  270.6 172.6 %copy-start.1 = (bf16[1,128,768]{2,1,0:T(8,128)(2,1)S(1)}, bf16[1,128,768]{2,1,0:T(8,128)(2,1)}, u32[]{:S(2)}) copy-start(bf16[1,128,768]{2,1,0:T(8,128)(2,1)} %param.8) | copy-start | bytes 589828
  270.6 184.4 %copy-start.4 = (bf16[768,64]{0,1:T(8,128)(2,1)S(1)}, bf16[768,64]{0,1:T(8,128)(2,1)}, u32[]{:S(2)}) copy-start(bf16[768,64]{0,1:T(8,128)(2,1)} %param.13) | copy-start | bytes 294916
  270.6 215.8 %copy-start.3 = (f32[128,64]{0,1:T(8,128)S(1)}, f32[128,64]{0,1:T(8,128)}, u32[]{:S(2)}) copy-start(f32[128,64]{0,1:T(8,128)} %param.14) | copy-start | bytes 98308
  444.5 42.6 %copy-start.2 = (bf16[128,768]{1,0:T(8,128)(2,1)}, bf16[128,768]{1,0:T(8,128)(2,1)S(1)}, u32[]{:S(2)}) copy-start(bf16[128,768]{1,0:T(8,128)(2,1)S(1)} %get-tuple-element.18) | copy-start | bytes 589828
Sparse Core Ops, SparseCore 0:
  25.8 94.2 all-gather.1
  129.2 129.5 all-reduce.4
  270.8 172.3 reduce-scatter.1
where the time goes:
time: 494 us
  waiting for transfers between devices  391 us (79%)
  blocking collectives  52.4 us (11%)
  matrix products  21.1 us (4%)
  between operations  15.9 us (3%)
  other arithmetic  12.5 us (3%)
    reduce_scatter x1, waiting for transfers between devices, on_device(): lax.psum_scatter(jnp.dot(activated, contract_weight, preferred_element_ty...  167 us
    psum x1, waiting for transfers between devices, on_device(): hidden_pre = lax.psum(hidden_part, 'narrow')  130 us
    all_gather x1, waiting for transfers between devices, on_device(): lax.all_gather(normed, 'wide', axis=0, tiled=True)  94.3 us
    psum x1, blocking collectives, on_device(): guided = lax.psum(velocity_part * copy_weight, ('cfg', 'narrow'))  31.1 us
    psum x2, blocking collectives, feature_norm(): lax.psum((jnp.sum(values, -1, keepdims=True), jnp.sum(values * values, -1...  21.2 us
    dot_general x1, matrix products, on_device(): jnp.dot(activated, contract_weight, preferred_element_type=jnp.float32)  11.8 us
  transfers between devices with their start and end apart: 3, of which 3 were waited for; matrix products, arithmetic and copies ran while one was open for 1% of the time, Pallas kernels for 0%

commit v1 on v0

--- a/solution.py
+++ b/solution.py
@@ -50,7 +50,7 @@
         expand_weight,
         preferred_element_type=jnp.float32,
     )
-    hidden_pre = lax.psum(hidden_part, "narrow")
+    hidden_pre = jnp.sum(lax.all_gather(hidden_part, "narrow"), axis=0)
     activated = jax.nn.gelu(hidden_pre, approximate=True).astype(jnp.bfloat16)
     ff_result = lax.psum_scatter(
         jnp.dot(activated, contract_weight, preferred_element_type=jnp.float32),

time: 494 us -> 602 us (1.22)
  waiting for transfers between devices: 391 us -> 487 us
  other arithmetic: 12.5 us -> 25.3 us
    all_gather x0 -> x1, waiting for transfers between devices: none -> 224 us  [on_device(): hidden_pre = jnp.sum(lax.all_gather(hidden_part, 'narrow'), axis=0)]
    psum x1 -> x0, waiting for transfers between devices: 130 us -> none  [on_device(): hidden_pre = lax.psum(hidden_part, 'narrow')]
    reduce_sum x0 -> x1, other arithmetic: none -> 12.5 us  [on_device(): hidden_pre = jnp.sum(lax.all_gather(hidden_part, 'narrow'), axis=0)]
where the time goes in v1:
time: 602 us
  waiting for transfers between devices  487 us (81%)
  blocking collectives  52.4 us (9%)
  other arithmetic  25.3 us (4%)
  matrix products  21.1 us (4%)
  between operations  15.9 us (3%)
    all_gather x1, waiting for transfers between devices, on_device(): hidden_pre = jnp.sum(lax.all_gather(hidden_part, 'narrow'), axis=0)  224 us
    reduce_scatter x1, waiting for transfers between devices, on_device(): lax.psum_scatter(jnp.dot(activated, contract_weight, preferred_element_ty...  168 us
    all_gather x1, waiting for transfers between devices, on_device(): lax.all_gather(normed, 'wide', axis=0, tiled=True)  94.3 us
    psum x1, blocking collectives, on_device(): guided = lax.psum(velocity_part * copy_weight, ('cfg', 'narrow'))  31.2 us
    psum x2, blocking collectives, feature_norm(): lax.psum((jnp.sum(values, -1, keepdims=True), jnp.sum(values * values, -1...  21.2 us
    reduce_sum x1, other arithmetic, on_device(): hidden_pre = jnp.sum(lax.all_gather(hidden_part, 'narrow'), axis=0)  12.5 us
  transfers between devices with their start and end apart: 3, of which 3 were waited for; matrix products, arithmetic and copies ran while one was open for 1% of the time, Pallas kernels for 0%

profile of v1, /device:TPU:2, one launch (start us, length us, event | category | flops | bytes accessed | tf_op | source)
XLA Modules:
  0.0 601.7 jit_solution(1549023992851632403)
XLA Ops:
  7.2 0.0 copy-start
  7.2 0.0 all-gather.4.cloned.1.call-start
  7.2 1.1 convert_reduce_fusion.1
  8.3 1.1 fusion.21
  9.4 1.1 add_reduce_fusion
  10.5 1.4 fusion.34
  11.9 1.3 compare_and_fusion.1
  13.2 10.7 %all-reduce.2 = (f32[128,1]{0,1:T(1,128)S(1)}, f32[128,1]{0,1:T(1,128)S(1)}) all-reduce(f32[128,1]{0,1:T(1,128)S(1)} %bitcast.50, f32[128,1]{0,1:T(1,128)S(1)} %bitcast.49), channel_id=1, replica_groups=mesh['cfg'=2,'wide'=32,'narrow'=4] {'narrow'}, use_global_device_ids=true, to_apply=%region_5.6 | all-reduce | flops 256 | bytes 2048 | tf_op jit(solution)/shard_map/psum | solution.py:21
  24.0 1.8 fusion.20
  25.8 0.0 all-gather.4.cloned.1.call-update
  25.8 0.0 all-gather.6.cloned.1.call-start
  25.9 94.3 %all-gather.4.cloned.1.call-done = bf16[4096,768]{1,0:T(8,128)(2,1)} async-done(((bf16[128,768]{1,0:T(8,128)(2,1)}), bf16[4096,768]{1,0:T(8,128)(2,1)}) %all-gather.4.cloned.1.call-update) | async-done | bytes 6291472 | tf_op jit(solution)/shard_map/all_gather | solution.py:49
  120.2 9.0 %fusion.41 = f32[4096,384]{1,0:T(8,128)} fusion(bf16[4096,768]{1,0:T(8,128)(2,1)} %all-gather.4.cloned.1.call-done, bf16[768,384]{1,0:T(8,128)(2,1)} %param.11), kind=kOutput, calls=%fused_computation.70 | convolution fusion | flops 2415919104 | bytes 13172736 | tf_op jit(solution)/shard_map/dot_general | solution.py:48
  129.2 0.0 all-gather.6.cloned.1.call-update
  129.2 0.0 reduce-scatter.2.cloned.1.call-start
  129.3 224.0 %all-gather.6.cloned.1.call-done = f32[16384,384]{1,0:T(8,128)} async-done(((f32[4096,384]{1,0:T(8,128)}), f32[16384,384]{1,0:T(8,128)}) %all-gather.6.cloned.1.call-update) | async-done | bytes 25165840 | tf_op jit(solution)/shard_map/all_gather | solution.py:53
  353.3 12.5 %reduce_sum.76 = f32[4096,384]{1,0:T(8,128)} reduce(f32[4,4096,384]{2,1,0:T(8,128)} %bitcast.47, f32[]{:T(128)} %constant.21.clone.1), dimensions={0}, to_apply=%region_6.7 | reduce | flops 4718592 | bytes 31457284 | tf_op jit(solution)/shard_map/reduce_sum | solution.py:53
  365.9 0.0 copy-done
  365.9 11.8 %fusion.8 = f32[4096,768]{1,0:T(8,128)} fusion(bf16[384,768]{1,0:T(8,128)(2,1)S(1)} %copy-done, f32[4096,384]{1,0:T(8,128)} %reduce_sum.76), kind=kOutput, calls=%fused_computation.9 | convolution fusion | flops 2430074880 | bytes 19464192 | tf_op jit(solution)/shard_map/dot_general | solution.py:56
  377.7 0.0 copy-start.1
  377.7 0.0 copy-start.4
  377.7 0.0 copy-start.3
  377.7 0.0 reduce-scatter.2.cloned.1.call-update
  377.7 0.3 reduce-window.9
  378.0 0.1 slice.40
  378.8 0.1 slice_reduce_fusion
  378.9 0.1 multiply_bitcast_fusion
  378.9 0.7 select_reduce_fusion
  381.0 0.7 iota_compare_fusion.1
  381.7 1.3 compare_and_fusion
  383.1 168.3 %reduce-scatter.2.cloned.1.call-done = f32[128,768]{1,0:T(8,128)} async-done(((f32[4096,768]{1,0:T(8,128)}), f32[128,768]{1,0:T(8,128)}) %reduce-scatter.2.cloned.1.call-update) | async-done | bytes 393232 | tf_op jit(solution)/shard_map/reduce_scatter | solution.py:55
  551.4 0.0 copy-done.1
  551.4 1.3 convert_reduce_fusion
  552.6 0.0 copy-start.2
  552.6 10.4 %all-reduce.1 = (f32[128,1]{0,1:T(1,128)S(1)}, f32[128,1]{0,1:T(1,128)S(1)}) all-reduce(f32[128,1]{0,1:T(1,128)S(1)} %bitcast.52, f32[128,1]{0,1:T(1,128)S(1)} %bitcast.51), channel_id=1, replica_groups=mesh['cfg'=2,'wide'=32,'narrow'=4] {'narrow'}, use_global_device_ids=true, to_apply=%region_14.15 | all-reduce | flops 256 | bytes 2048 | tf_op jit(solution)/shard_map/psum | solution.py:21
  563.1 0.0 copy-done.4
  563.1 0.3 convolution_multiply_fusion
  563.4 31.2 %psum.39 = f32[128,64]{0,1:T(8,128)S(1)} all-reduce(f32[128,64]{0,1:T(8,128)S(1)} %convolution_multiply_fusion), channel_id=1, replica_groups=mesh['cfg'=2,'wide'=32,'narrow'=4] {'cfg','narrow'}, use_global_device_ids=true, to_apply=%region_15.16 | all-reduce | flops 8192 | bytes 65536 | tf_op jit(solution)/shard_map/psum | solution.py:66
  594.5 0.0 copy-done.3
  594.6 0.6 subtract_select_fusion
  595.2 0.0 copy-done.2
  (5 shorter events, 0.1 us)
Async XLA Ops:
  7.2 358.7 %copy-start = (bf16[384,768]{1,0:T(8,128)(2,1)S(1)}, bf16[384,768]{1,0:T(8,128)(2,1)}, u32[]{:S(2)}) copy-start(bf16[384,768]{1,0:T(8,128)(2,1)} %param.12) | copy-start | bytes 1769476
  7.2 113.0 %all-gather.4.cloned.1.call-start = ((), (), s32[]{:S(2)}) async-start(), calls=%async_computation.1 | async-start | bytes 6488064 | tf_op jit(solution)/shard_map/all_gather | solution.py:49
  25.8 327.5 %all-gather.6.cloned.1.call-start = ((), (), s32[]{:S(2)}) async-start(), calls=%async_computation.3 | async-start | bytes 31457280 | tf_op jit(solution)/shard_map/all_gather | solution.py:53
  129.2 422.1 %reduce-scatter.2.cloned.1.call-start = ((), (), s32[]{:S(2)}) async-start(), calls=%async_computation.2 | async-start | bytes 12976128 | tf_op jit(solution)/shard_map/reduce_scatter | solution.py:55
  377.7 173.7 %copy-start.1 = (bf16[1,128,768]{2,1,0:T(8,128)(2,1)S(1)}, bf16[1,128,768]{2,1,0:T(8,128)(2,1)}, u32[]{:S(2)}) copy-start(bf16[1,128,768]{2,1,0:T(8,128)(2,1)} %param.8) | copy-start | bytes 589828
  377.7 185.4 %copy-start.4 = (bf16[768,64]{0,1:T(8,128)(2,1)S(1)}, bf16[768,64]{0,1:T(8,128)(2,1)}, u32[]{:S(2)}) copy-start(bf16[768,64]{0,1:T(8,128)(2,1)} %param.13) | copy-start | bytes 294916
  377.7 216.9 %copy-start.3 = (f32[128,64]{0,1:T(8,128)S(1)}, f32[128,64]{0,1:T(8,128)}, u32[]{:S(2)}) copy-start(f32[128,64]{0,1:T(8,128)} %param.14) | copy-start | bytes 98308
  552.6 42.6 %copy-start.2 = (bf16[128,768]{1,0:T(8,128)(2,1)}, bf16[128,768]{1,0:T(8,128)(2,1)S(1)}, u32[]{:S(2)}) copy-start(bf16[128,768]{1,0:T(8,128)(2,1)S(1)} %get-tuple-element.18) | copy-start | bytes 589828
Sparse Core Ops, SparseCore 0:
  25.9 94.2 all-gather.3
  129.4 223.9 all-gather.5
  377.8 173.4 reduce-scatter.1
